TPU v7x, 128 devices: a whole 4x4x4 slice. The times are simulated.
128 devices in a mesh: tok: 8 (over x, z_hi), feat: 16 (over y, z_lo, core).
Axes of the slice: x: 4, y: 4, z: 4 (z_hi: 2, z_lo: 2; z = z_hi * 2 + z_lo), core: 2. Of those that a mesh axis runs over, the one named last changes fastest.
Arguments:
- resid: bfloat16 [2048, 8192], P(None, ('tok', 'feat')), may hold values from -6 to 6
- resid_grad: bfloat16 [2048, 8192], P(None, ('tok', 'feat')), may hold values from -6 to 6
- active: int32 [16, 20], P('tok'), may hold values from 0 to 79, all different within a row
- w_enc: bfloat16 [8192, 10240], P(None, 'feat'), may hold values from -0.0625 to 0.0625
- b_enc: float32 [10240], P('feat'), may hold values from -3 to 3
- w_dec: bfloat16 [10240, 8192], P('feat'), may hold values from -0.25 to 0.25
- b_dec: float32 [8192], P('feat'), may hold values from -3 to 3
Outputs:
- feature_attr: float32 [2048, 10240], P('tok', 'feat')
- error: float32 [2048, 8192], P('tok', 'feat')
- error_attr: float32 [2048], P('tok')
Inputs may be any that keep to these rules, and one draw needn't show every extreme that they name: `active`: each row lists 20 different feature blocks; every block is listed by some tile.
All inputs are finite; a program needn't handle non-finite values.
Results may differ from a plain program's by a relative error of at most 0.012.
Values may be sent and summed in bfloat16 or wider, within the bound.
A program may use at most 128 MiB of HBM per device.

v0:
```python
import jax
import jax.numpy as jnp
from jax import lax
from jax.sharding import PartitionSpec as P

BLOCK = 128
TILE = 128


def per_device(resid, resid_grad, active, w_enc, b_enc, w_dec, b_dec):
    n_feat = lax.axis_size("feat")
    width = resid.shape[1]
    cols_x, cols_g = (
        lax.all_gather(resid[:, None, :], "feat", axis=1, tiled=True),
        lax.all_gather(resid_grad[:, None, :], "feat", axis=1, tiled=True),
    )
    total = cols_x.shape[0]
    cols_x = cols_x.reshape(total, n_feat * width)
    cols_g = cols_g.reshape(total, n_feat * width)
    rows_x, rows_g = (
        lax.all_to_all(cols_x, "tok", split_axis=0, concat_axis=1, tiled=True),
        lax.all_to_all(cols_g, "tok", split_axis=0, concat_axis=1, tiled=True),
    )
    tok_rows = rows_x.shape[0]
    feat_dev = w_enc.shape[1]
    blocks = feat_dev // BLOCK
    tiles_dev = active.shape[0]
    block_ids = lax.axis_index("feat") * blocks + jnp.arange(blocks, dtype=jnp.int32)
    hits = jnp.any(active[:, :, None] == block_ids[None, None, :], axis=1).astype(jnp.float32)
    pre = jnp.dot(rows_x, w_enc, preferred_element_type=jnp.float32) + b_enc
    shaped = jnp.maximum(pre, 0.0).reshape(tiles_dev, TILE, blocks, BLOCK) * hits[:, None, :, None]
    acts = shaped.reshape(tok_rows, feat_dev).astype(jnp.bfloat16)
    partial_recon = jnp.dot(acts, w_dec, preferred_element_type=jnp.float32)
    recon_share = lax.psum_scatter(
        partial_recon.astype(jnp.bfloat16), "feat", scatter_dimension=1, tiled=True
    ).astype(jnp.float32)
    share = recon_share.shape[1]
    start = lax.axis_index("feat") * share
    own_x = lax.dynamic_slice_in_dim(rows_x, start, share, 1)
    own_g = lax.dynamic_slice_in_dim(rows_g, start, share, 1)
    recon = recon_share + b_dec
    error = own_x.astype(jnp.float32) - recon
    local_terms = jnp.sum(error * own_g.astype(jnp.float32), axis=1)
    error_attr = lax.psum(local_terms, "feat")
    proj = lax.dot_general(
        rows_g, w_dec, (((1,), (1,)), ((), ())), preferred_element_type=jnp.float32
    )
    feature_attr = acts.astype(jnp.float32) * proj
    return (feature_attr, error, error_attr)


def solution(mesh):
    placed = (
        P(None, ("tok", "feat")),
        P(None, ("tok", "feat")),
        P("tok", None),
        P(None, "feat"),
        P("feat"),
        P("feat", None),
        P("feat"),
    )
    return jax.shard_map(
        per_device,
        mesh=mesh,
        in_specs=placed,
        out_specs=(P("tok", "feat"), P("tok", "feat"), P("tok")),
        check_vma=False,
    )
```

profile of v0, /device:TPU:0, one launch (start us, length us, event | category | flops | bytes accessed | tf_op | source)
XLA Modules:
  0.0 284.6 jit_solution(3607693962824944712)
XLA Ops:
  7.2 0.0 all-gather.5.cloned.1.call-start
  7.2 0.7 all-gather.5.cloned.1.call-update
  7.9 0.0 all-gather.7.cloned.1.call-start
  7.9 0.7 all-gather.7.cloned.1.call-update
  8.6 40.8 %all-gather.5.cloned.1.call-done = bf16[2048,1024]{0,1:T(8,128)(2,1)} async-done(((bf16[2048,64]{0,1:T(8,128)(2,1)}), bf16[2048,1024]{0,1:T(8,128)(2,1)}) %all-gather.5.cloned.1.call-update) | async-done | bytes 4194320 | tf_op jit(solution)/shard_map/all_gather | solution.py:14
  49.5 6.4 %copy.20 = bf16[2048,1024]{1,0:T(8,128)(2,1)} copy(bf16[2048,1024]{0,1:T(8,128)(2,1)} %all-gather.5.cloned.1.call-done) | data formatting | bytes 8388608 | tf_op jit(solution)/shard_map/all_gather | solution.py:14
  55.8 0.0 copy-start.3
  55.8 6.6 %all-to-all-start = ((bf16[8,256,1024]{2,1,0:T(8,128)(2,1)}), bf16[8,256,1024]{2,1,0:T(8,128)(2,1)}, u32[]{:S(2)}, u32[]{:S(2)}) async-start(bf16[8,256,1024]{2,1,0:T(8,128)(2,1)} %bitcast.21), calls=%async_computation | async-start | bytes 8388608 | tf_op jit(solution)/shard_map/all_to_all | solution.py:21
  62.5 0.0 reduce-scatter.2.cloned.1.call-start
  62.5 0.0 copy-done.3
  62.5 0.2 compare_reduce_fusion
  62.7 0.1 copy.22
  62.8 0.2 mul.24
  63.1 0.2 copy.23
  63.4 59.7 %all-to-all-done = bf16[8,256,1024]{2,1,0:T(8,128)(2,1)} async-done(((bf16[8,256,1024]{2,1,0:T(8,128)(2,1)}), bf16[8,256,1024]{2,1,0:T(8,128)(2,1)}, u32[]{:S(2)}, u32[]{:S(2)}) %all-to-all-start) | async-done | bytes 4194336 | tf_op jit(solution)/shard_map/all_to_all | solution.py:21
  123.1 0.0 copy-start.4
  123.1 0.0 slice-start
  123.1 2.9 %copy.26 = bf16[8,32,8,1024]{3,2,0,1:T(8,128)(2,1)S(1)} copy(bf16[8,32,8,1024]{3,2,1,0:T(8,128)(2,1)} %bitcast.4) | data formatting | bytes 8388608 | tf_op jit(solution)/shard_map/all_to_all | solution.py:21
  126.0 0.0 copy-start
  126.0 2.0 copy-done
  127.9 0.0 copy-done.4
  127.9 0.0 slice-start.1
  127.9 0.0 slice-start.2
  127.9 6.5 %fusion.2 = bf16[256,640]{1,0:T(8,128)(2,1)S(1)} fusion(f32[256,640]{1,0:T(8,128)S(1)} %copy.23, bf16[256,8192]{1,0:T(8,128)(2,1)S(1)} %bitcast.23, bf16[8192,640]{1,0:T(8,128)(2,1)} %param.10, f32[640]{0:T(1024)S(1)} %copy-done.4), kind=kOutput, calls=%fused_computation.5 | convolution fusion | flops 2685009920 | bytes 15665664 | tf_op jit(solution)/shard_map/dot_general | solution.py:30
  134.4 0.0 slice-done
  134.4 0.0 slice-done.1
  134.4 0.0 slice-done.2
  134.4 4.9 %convolution_convert_fusion = bf16[256,8192]{1,0:T(8,128)(2,1)} fusion(bf16[256,640]{1,0:T(8,128)(2,1)S(1)} %fusion.2, bf16[640,8192]{1,0:T(8,128)(2,1)S(1)} %bitcast.30), kind=kOutput, calls=%fused_computation | convolution fusion | flops 2686451712 | bytes 15007744 | tf_op jit(solution)/shard_map/dot_general | solution.py:33
  139.4 0.0 reduce-scatter.2.cloned.1.call-update
  139.4 0.0 all-gather.7.cloned.1.call-done
  139.4 6.4 %copy.24 = bf16[2048,1024]{1,0:T(8,128)(2,1)} copy(bf16[2048,1024]{0,1:T(8,128)(2,1)} %all-gather.7.cloned.1.call-done) | data formatting | bytes 8388608 | tf_op jit(solution)/shard_map/all_gather | solution.py:15
  145.8 4.8 %all-to-all-start.1 = ((bf16[8,256,1024]{2,1,0:T(8,128)(2,1)}), bf16[8,256,1024]{2,1,0:T(8,128)(2,1)}, u32[]{:S(2)}, u32[]{:S(2)}) async-start(bf16[8,256,1024]{2,1,0:T(8,128)(2,1)} %bitcast.22), calls=%async_computation.1 | async-start | bytes 8388608 | tf_op jit(solution)/shard_map/all_to_all | solution.py:22
  150.6 61.9 %all-to-all-done.1 = bf16[8,256,1024]{2,1,0:T(8,128)(2,1)} async-done(((bf16[8,256,1024]{2,1,0:T(8,128)(2,1)}), bf16[8,256,1024]{2,1,0:T(8,128)(2,1)}, u32[]{:S(2)}, u32[]{:S(2)}) %all-to-all-start.1) | async-done | bytes 4194336 | tf_op jit(solution)/shard_map/all_to_all | solution.py:22
  212.5 2.7 copy.27
  215.2 0.0 copy-start.1
  215.2 1.9 copy-done.1
  217.1 0.0 copy-start.2
  217.1 7.1 %convolution_multiply_fusion = f32[256,640]{1,0:T(8,128)} fusion(bf16[256,8192]{1,0:T(8,128)(2,1)S(1)} %bitcast.25, bf16[640,8192]{1,0:T(8,128)(2,1)} %param.12, bf16[256,640]{1,0:T(8,128)(2,1)S(1)} %fusion.2), kind=kOutput, calls=%fused_computation.1 | convolution fusion | flops 2684682240 | bytes 15663104 | tf_op jit(solution)/shard_map/dot_general | solution.py:45
  224.2 22.1 %reduce-scatter.2.cloned.1.call-done = bf16[256,512]{1,0:T(8,128)(2,1)} async-done(((bf16[256,8192]{1,0:T(8,128)(2,1)}), bf16[256,512]{1,0:T(8,128)(2,1)}) %reduce-scatter.2.cloned.1.call-update) | async-done | bytes 262160 | tf_op jit(solution)/shard_map/reduce_scatter | solution.py:34
  246.3 0.0 copy-done.2
  246.3 2.0 multiply_reduce_fusion
  248.3 29.7 %psum.7 = f32[256]{0:T(256)} all-reduce(f32[256]{0:T(256)S(1)} %get-tuple-element.3), channel_id=1, replica_groups=mesh['tok'=8,'feat'=16] {'feat'}, use_global_device_ids=true, to_apply=%region_3.0 | all-reduce | flops 256 | bytes 2048 | tf_op jit(solution)/shard_map/psum | solution.py:44
  (4 shorter events, 0.1 us)
Async XLA Ops:
  7.2 42.3 %all-gather.5.cloned.1.call-start = ((), (), s32[]{:S(2)}) async-start(), calls=%async_computation.4 | async-start | bytes 4456448 | tf_op jit(solution)/shard_map/all_gather | solution.py:14
  7.9 131.5 %all-gather.7.cloned.1.call-start = ((), (), s32[]{:S(2)}) async-start(), calls=%async_computation.5 | async-start | bytes 4456448 | tf_op jit(solution)/shard_map/all_gather | solution.py:15
  55.8 6.7 %copy-start.3 = (s32[2,20]{1,0:T(2,128)S(1)}, s32[2,20]{1,0:T(2,128)}, u32[]{:S(2)}) copy-start(s32[2,20]{1,0:T(2,128)} %param.9) | copy-start | bytes 484
  55.8 67.2 %all-to-all-start = ((bf16[8,256,1024]{2,1,0:T(8,128)(2,1)}), bf16[8,256,1024]{2,1,0:T(8,128)(2,1)}, u32[]{:S(2)}, u32[]{:S(2)}) async-start(bf16[8,256,1024]{2,1,0:T(8,128)(2,1)} %bitcast.21), calls=%async_computation | async-start | bytes 8388608 | tf_op jit(solution)/shard_map/all_to_all | solution.py:21
  62.5 183.8 %reduce-scatter.2.cloned.1.call-start = ((), (), s32[]{:S(2)}) async-start(), calls=%async_computation.3 | async-start | bytes 4456448 | tf_op jit(solution)/shard_map/reduce_scatter | solution.py:34
  123.1 4.9 %copy-start.4 = (f32[640]{0:T(1024)S(1)}, f32[640]{0:T(1024)}, u32[]{:S(2)}) copy-start(f32[640]{0:T(1024)} %param.11) | copy-start | bytes 7684
  123.1 11.3 %slice-start = ((s8[10485760]{0:T(1024)(128)(4,1)}), s8[4194304]{0:T(1024)(128)(4,1)S(1)}, s32[]{:S(2)}) async-start(s8[10485760]{0:T(1024)(128)(4,1)} %bitcast.29), calls=%async_computation.6 | async-start | bytes 8388608
  126.0 2.0 copy-start
  127.9 6.5 %slice-start.1 = ((s8[10485760]{0:T(1024)(128)(4,1)}), s8[4194304]{0:T(1024)(128)(4,1)S(1)}, s32[]{:S(2)}) async-start(s8[10485760]{0:T(1024)(128)(4,1)} %bitcast.29), calls=%async_computation.7 | async-start | bytes 8388608
  127.9 6.5 %slice-start.2 = ((s8[10485760]{0:T(1024)(128)(4,1)}), s8[2097152]{0:T(1024)(128)(4,1)S(1)}, s32[]{:S(2)}) async-start(s8[10485760]{0:T(1024)(128)(4,1)} %bitcast.29), calls=%async_computation.8 | async-start | bytes 4194304
  145.8 66.7 %all-to-all-start.1 = ((bf16[8,256,1024]{2,1,0:T(8,128)(2,1)}), bf16[8,256,1024]{2,1,0:T(8,128)(2,1)}, u32[]{:S(2)}, u32[]{:S(2)}) async-start(bf16[8,256,1024]{2,1,0:T(8,128)(2,1)} %bitcast.22), calls=%async_computation.1 | async-start | bytes 8388608 | tf_op jit(solution)/shard_map/all_to_all | solution.py:22
  215.2 1.9 copy-start.1
  217.1 29.2 %copy-start.2 = (f32[512]{0:T(512)S(1)}, f32[512]{0:T(512)}, u32[]{:S(2)}) copy-start(f32[512]{0:T(512)} %param.13) | copy-start | bytes 6148
Sparse Core Ops, SparseCore 0:
  9.7 39.7 all-gather.4
  51.2 79.7 all-gather.6
  139.5 106.7 reduce-scatter.1
where the time goes:
time: 285 us
  waiting for transfers between devices  186 us (65%)
  blocking collectives  29.7 us (10%)
  local copies, waits for them, and re-layouts  22.8 us (8%)
  matrix products  18.5 us (6%)
  between operations  13.9 us (5%)
  starting transfers between devices  11.6 us (4%)
    all_to_all x1, waiting for transfers between devices, per_device(): lax.all_to_all(cols_g, 'tok', split_axis=0, concat_axis=1, tiled=True)  61.9 us
    all_to_all x1, waiting for transfers between devices, per_device(): lax.all_to_all(cols_x, 'tok', split_axis=0, concat_axis=1, tiled=True)  59.7 us
    all_gather x1, waiting for transfers between devices, per_device(): lax.all_gather(resid[:, None, :], 'feat', axis=1, tiled=True)  40.8 us
    psum x1, blocking collectives, per_device(): error_attr = lax.psum(local_terms, 'feat')  29.7 us
    reduce_scatter x1, waiting for transfers between devices, per_device(): lax.psum_scatter(partial_recon.astype(jnp.bfloat16), 'feat', scatter_dime...  22.1 us
    dot_general x1, matrix products, per_device(): lax.dot_general(rows_g, w_dec, (((1,), (1,)), ((), ())), preferred_elemen...  7.11 us
    all_to_all x1, starting transfers between devices, per_device(): lax.all_to_all(cols_x, 'tok', split_axis=0, concat_axis=1, tiled=True)  6.65 us
    dot_general x1, matrix products, per_device(): pre = jnp.dot(rows_x, w_enc, preferred_element_type=jnp.float32) + b_enc  6.46 us
  transfers between devices with their start and end apart: 5, of which 4 were waited for; matrix products, arithmetic and copies ran while one was open for 13% of the time, Pallas kernels for 0%

commit v1 on v0

--- a/solution.py
+++ b/solution.py
@@ -41,7 +41,7 @@
     recon = recon_share + b_dec
     error = own_x.astype(jnp.float32) - recon
     local_terms = jnp.sum(error * own_g.astype(jnp.float32), axis=1)
-    error_attr = lax.psum(local_terms, "feat")
+    error_attr = jnp.sum(lax.all_gather(local_terms, "feat"), axis=0)
     proj = lax.dot_general(
         rows_g, w_dec, (((1,), (1,)), ((), ())), preferred_element_type=jnp.float32
     )

time: 285 us -> 273 us (0.958)
  blocking collectives: 29.7 us -> 16 us
    psum x1 -> x0, blocking collectives: 29.7 us -> none  [per_device(): error_attr = lax.psum(local_terms, 'feat')]
    all_gather x0 -> x1, blocking collectives: none -> 16 us  [per_device(): error_attr = jnp.sum(lax.all_gather(local_terms, 'feat'), axis=0)]
  transfers between devices with their start and end apart: 5 -> 5, of which waited for: 4 -> 4; matrix products, arithmetic and copies ran while one was open for 13% -> 14% of each run, Pallas kernels for 0% -> 0%
where the time goes in v1:
time: 273 us; the launch traced here: 272 us
  waiting for transfers between devices  186 us (68%)
  local copies, waits for them, and re-layouts  22.8 us (8%)
  matrix products  18.6 us (7%)
  blocking collectives  16 us (6%)
  between operations  13.9 us (5%)
  starting transfers between devices  11.6 us (4%)
  other arithmetic  2.81 us (1%)
    all_to_all x1, waiting for transfers between devices, per_device(): lax.all_to_all(cols_g, 'tok', split_axis=0, concat_axis=1, tiled=True)  61.6 us
    all_to_all x1, waiting for transfers between devices, per_device(): lax.all_to_all(cols_x, 'tok', split_axis=0, concat_axis=1, tiled=True)  59.7 us
    all_gather x1, waiting for transfers between devices, per_device(): lax.all_gather(resid[:, None, :], 'feat', axis=1, tiled=True)  40.8 us
    reduce_scatter x1, waiting for transfers between devices, per_device(): lax.psum_scatter(partial_recon.astype(jnp.bfloat16), 'feat', scatter_dime...  22.5 us
    all_gather x1, blocking collectives, per_device(): error_attr = jnp.sum(lax.all_gather(local_terms, 'feat'), axis=0)  16 us
    dot_general x1, matrix products, per_device(): lax.dot_general(rows_g, w_dec, (((1,), (1,)), ((), ())), preferred_elemen...  7.11 us
    all_to_all x1, starting transfers between devices, per_device(): lax.all_to_all(cols_x, 'tok', split_axis=0, concat_axis=1, tiled=True)  6.65 us
    dot_general x1, matrix products, per_device(): pre = jnp.dot(rows_x, w_enc, preferred_element_type=jnp.float32) + b_enc  6.46 us
  transfers between devices with their start and end apart: 5, of which 4 were waited for; matrix products, arithmetic and copies ran while one was open for 14% of the time, Pallas kernels for 0%

profile of v1, /device:TPU:0, one launch (start us, length us, event | category | flops | bytes accessed | tf_op | source)
XLA Modules:
  0.0 271.6 jit_solution(2767278541426732856)
XLA Ops:
  7.2 0.0 all-gather.7.cloned.1.call-start
  7.2 0.7 all-gather.7.cloned.1.call-update
  7.9 0.0 all-gather.9.cloned.1.call-start
  7.9 0.7 all-gather.9.cloned.1.call-update
  8.6 40.8 %all-gather.7.cloned.1.call-done = bf16[2048,1024]{0,1:T(8,128)(2,1)} async-done(((bf16[2048,64]{0,1:T(8,128)(2,1)}), bf16[2048,1024]{0,1:T(8,128)(2,1)}) %all-gather.7.cloned.1.call-update) | async-done | bytes 4194320 | tf_op jit(solution)/shard_map/all_gather | solution.py:14
  49.5 6.4 %copy.20 = bf16[2048,1024]{1,0:T(8,128)(2,1)} copy(bf16[2048,1024]{0,1:T(8,128)(2,1)} %all-gather.7.cloned.1.call-done) | data formatting | bytes 8388608 | tf_op jit(solution)/shard_map/all_gather | solution.py:14
  55.8 0.0 copy-start.3
  55.8 6.6 %all-to-all-start = ((bf16[8,256,1024]{2,1,0:T(8,128)(2,1)}), bf16[8,256,1024]{2,1,0:T(8,128)(2,1)}, u32[]{:S(2)}, u32[]{:S(2)}) async-start(bf16[8,256,1024]{2,1,0:T(8,128)(2,1)} %bitcast.22), calls=%async_computation | async-start | bytes 8388608 | tf_op jit(solution)/shard_map/all_to_all | solution.py:21
  62.5 0.0 reduce-scatter.2.cloned.1.call-start
  62.5 0.0 copy-done.3
  62.5 0.2 compare_reduce_fusion
  62.7 0.1 copy.22
  62.8 0.2 mul.24
  63.1 0.2 copy.23
  63.4 59.7 %all-to-all-done = bf16[8,256,1024]{2,1,0:T(8,128)(2,1)} async-done(((bf16[8,256,1024]{2,1,0:T(8,128)(2,1)}), bf16[8,256,1024]{2,1,0:T(8,128)(2,1)}, u32[]{:S(2)}, u32[]{:S(2)}) %all-to-all-start) | async-done | bytes 4194336 | tf_op jit(solution)/shard_map/all_to_all | solution.py:21
  123.1 0.0 copy-start.4
  123.1 0.0 slice-start
  123.1 2.9 %copy.26 = bf16[8,32,8,1024]{3,2,0,1:T(8,128)(2,1)S(1)} copy(bf16[8,32,8,1024]{3,2,1,0:T(8,128)(2,1)} %bitcast.5) | data formatting | bytes 8388608 | tf_op jit(solution)/shard_map/all_to_all | solution.py:21
  126.0 0.0 copy-start
  126.0 2.0 copy-done
  127.9 0.0 copy-done.4
  127.9 0.0 slice-start.1
  127.9 0.0 slice-start.2
  127.9 6.5 %fusion.2 = bf16[256,640]{1,0:T(8,128)(2,1)S(1)} fusion(f32[256,640]{1,0:T(8,128)S(1)} %copy.23, bf16[256,8192]{1,0:T(8,128)(2,1)S(1)} %bitcast.24, bf16[8192,640]{1,0:T(8,128)(2,1)} %param.10, f32[640]{0:T(1024)S(1)} %copy-done.4), kind=kOutput, calls=%fused_computation.5 | convolution fusion | flops 2685009920 | bytes 15665664 | tf_op jit(solution)/shard_map/dot_general | solution.py:30
  134.4 0.0 slice-done
  134.4 0.0 slice-done.1
  134.4 0.0 slice-done.2
  134.4 5.0 %convolution_convert_fusion = bf16[256,8192]{1,0:T(8,128)(2,1)} fusion(bf16[256,640]{1,0:T(8,128)(2,1)S(1)} %fusion.2, bf16[640,8192]{1,0:T(8,128)(2,1)S(1)} %bitcast.32), kind=kOutput, calls=%fused_computation | convolution fusion | flops 2686451712 | bytes 15007744 | tf_op jit(solution)/shard_map/dot_general | solution.py:33
  139.5 0.0 reduce-scatter.2.cloned.1.call-update
  139.5 0.0 all-gather.9.cloned.1.call-done
  139.5 6.4 %copy.24 = bf16[2048,1024]{1,0:T(8,128)(2,1)} copy(bf16[2048,1024]{0,1:T(8,128)(2,1)} %all-gather.9.cloned.1.call-done) | data formatting | bytes 8388608 | tf_op jit(solution)/shard_map/all_gather | solution.py:15
  145.9 4.8 %all-to-all-start.1 = ((bf16[8,256,1024]{2,1,0:T(8,128)(2,1)}), bf16[8,256,1024]{2,1,0:T(8,128)(2,1)}, u32[]{:S(2)}, u32[]{:S(2)}) async-start(bf16[8,256,1024]{2,1,0:T(8,128)(2,1)} %bitcast.23), calls=%async_computation.1 | async-start | bytes 8388608 | tf_op jit(solution)/shard_map/all_to_all | solution.py:22
  150.7 61.6 %all-to-all-done.1 = bf16[8,256,1024]{2,1,0:T(8,128)(2,1)} async-done(((bf16[8,256,1024]{2,1,0:T(8,128)(2,1)}), bf16[8,256,1024]{2,1,0:T(8,128)(2,1)}, u32[]{:S(2)}, u32[]{:S(2)}) %all-to-all-start.1) | async-done | bytes 4194336 | tf_op jit(solution)/shard_map/all_to_all | solution.py:22
  212.3 2.7 copy.27
  215.0 0.0 copy-start.1
  215.0 1.9 copy-done.1
  216.9 0.0 copy-start.2
  216.9 7.1 %convolution_multiply_fusion = f32[256,640]{1,0:T(8,128)} fusion(bf16[256,8192]{1,0:T(8,128)(2,1)S(1)} %bitcast.26, bf16[640,8192]{1,0:T(8,128)(2,1)} %param.12, bf16[256,640]{1,0:T(8,128)(2,1)S(1)} %fusion.2), kind=kOutput, calls=%fused_computation.1 | convolution fusion | flops 2684682240 | bytes 15663104 | tf_op jit(solution)/shard_map/dot_general | solution.py:45
  224.0 22.5 %reduce-scatter.2.cloned.1.call-done = bf16[256,512]{1,0:T(8,128)(2,1)} async-done(((bf16[256,8192]{1,0:T(8,128)(2,1)}), bf16[256,512]{1,0:T(8,128)(2,1)}) %reduce-scatter.2.cloned.1.call-update) | async-done | bytes 262160 | tf_op jit(solution)/shard_map/reduce_scatter | solution.py:34
  246.5 0.0 copy-done.2
  246.5 2.0 multiply_reduce_fusion
  248.5 16.0 %all-gather.3 = f32[16,1,256]{2,1,0:T(1,128)S(1)} all-gather(f32[1,1,256]{2,1,0:T(1,128)S(1)} %bitcast.30), channel_id=4, replica_groups=mesh['tok'=8,'feat'=16] {'feat'}, dimensions={0}, use_global_device_ids=true | all-gather | bytes 17408 | tf_op jit(solution)/shard_map/all_gather | solution.py:44
  264.5 0.6 reduce_sum.19
  (4 shorter events, 0.1 us)
Async XLA Ops:
  7.2 42.3 %all-gather.7.cloned.1.call-start = ((), (), s32[]{:S(2)}) async-start(), calls=%async_computation.4 | async-start | bytes 4456448 | tf_op jit(solution)/shard_map/all_gather | solution.py:14
  7.9 131.6 %all-gather.9.cloned.1.call-start = ((), (), s32[]{:S(2)}) async-start(), calls=%async_computation.5 | async-start | bytes 4456448 | tf_op jit(solution)/shard_map/all_gather | solution.py:15
  55.8 6.7 %copy-start.3 = (s32[2,20]{1,0:T(2,128)S(1)}, s32[2,20]{1,0:T(2,128)}, u32[]{:S(2)}) copy-start(s32[2,20]{1,0:T(2,128)} %param.9) | copy-start | bytes 484
  55.8 67.2 %all-to-all-start = ((bf16[8,256,1024]{2,1,0:T(8,128)(2,1)}), bf16[8,256,1024]{2,1,0:T(8,128)(2,1)}, u32[]{:S(2)}, u32[]{:S(2)}) async-start(bf16[8,256,1024]{2,1,0:T(8,128)(2,1)} %bitcast.22), calls=%async_computation | async-start | bytes 8388608 | tf_op jit(solution)/shard_map/all_to_all | solution.py:21
  62.5 184.0 %reduce-scatter.2.cloned.1.call-start = ((), (), s32[]{:S(2)}) async-start(), calls=%async_computation.3 | async-start | bytes 4456448 | tf_op jit(solution)/shard_map/reduce_scatter | solution.py:34
  123.1 4.9 %copy-start.4 = (f32[640]{0:T(1024)S(1)}, f32[640]{0:T(1024)}, u32[]{:S(2)}) copy-start(f32[640]{0:T(1024)} %param.11) | copy-start | bytes 7684
  123.1 11.3 %slice-start = ((s8[10485760]{0:T(1024)(128)(4,1)}), s8[4194304]{0:T(1024)(128)(4,1)S(1)}, s32[]{:S(2)}) async-start(s8[10485760]{0:T(1024)(128)(4,1)} %bitcast.31), calls=%async_computation.6 | async-start | bytes 8388608
  126.0 2.0 copy-start
  127.9 6.5 %slice-start.1 = ((s8[10485760]{0:T(1024)(128)(4,1)}), s8[4194304]{0:T(1024)(128)(4,1)S(1)}, s32[]{:S(2)}) async-start(s8[10485760]{0:T(1024)(128)(4,1)} %bitcast.31), calls=%async_computation.7 | async-start | bytes 8388608
  127.9 6.5 %slice-start.2 = ((s8[10485760]{0:T(1024)(128)(4,1)}), s8[2097152]{0:T(1024)(128)(4,1)S(1)}, s32[]{:S(2)}) async-start(s8[10485760]{0:T(1024)(128)(4,1)} %bitcast.31), calls=%async_computation.8 | async-start | bytes 4194304
  145.9 66.4 %all-to-all-start.1 = ((bf16[8,256,1024]{2,1,0:T(8,128)(2,1)}), bf16[8,256,1024]{2,1,0:T(8,128)(2,1)}, u32[]{:S(2)}, u32[]{:S(2)}) async-start(bf16[8,256,1024]{2,1,0:T(8,128)(2,1)} %bitcast.23), calls=%async_computation.1 | async-start | bytes 8388608 | tf_op jit(solution)/shard_map/all_to_all | solution.py:22
  215.0 1.9 copy-start.1
  216.9 29.6 %copy-start.2 = (f32[512]{0:T(512)S(1)}, f32[512]{0:T(512)}, u32[]{:S(2)}) copy-start(f32[512]{0:T(512)} %param.13) | copy-start | bytes 6148
Sparse Core Ops, SparseCore 0:
  9.7 39.7 all-gather.6
  51.2 79.7 all-gather.8
  139.6 106.8 reduce-scatter.1
